TPU v7x, 256 devices: a whole 4x4x8 slice. The times are simulated.
256 devices in a mesh: walker: 16 (over x, y), tangent: 8 (over z), feat: 2 (over core).
Axes of the slice: x: 4, y: 4, z: 8, core: 2. Of those that a mesh axis runs over, the one named last changes fastest.
Arguments:
- value_in: bfloat16 [512, 512], P('walker', 'feat'), may hold values from -0.94921875 to 0.94921875
- tang_in: bfloat16 [512, 768, 512], P('walker', 'tangent', 'feat'), may hold values from -1.01 to 1.01
- lap_in: bfloat16 [512, 512], P('walker', 'feat'), may hold values from -6 to 6
- w_first: bfloat16 [512, 512], P(('walker', 'tangent', 'feat')), may hold values from -0.25 to 0.25
- b_first: float32 [512], replicated, may hold values from -3 to 3
- w_second: bfloat16 [512, 512], P(('walker', 'tangent', 'feat')), may hold values from -0.25 to 0.25
- b_second: float32 [512], replicated, may hold values from -3 to 3
- readout: float32 [512], replicated, may hold values from -0.6 to 0.6
Outputs:
- log_amplitude: float32 [512], P('walker')
- gradient: float32 [512, 768], P('walker', 'tangent')
- kinetic: float32 [512], P('walker')
All inputs are finite; a program needn't handle non-finite values.
Results may differ from a plain program's by a relative error of at most 0.0044.
Values may be sent and summed in bfloat16 or wider, within the bound.
No kernel may reach another device: no remote copies, remote signals or barrier semaphores. Data moves between devices by JAX's collectives and lax.ppermute only.
A program may use at most 64 MiB of HBM per device.

v0:
```python
import jax
import jax.numpy as jnp
from jax import lax
from jax.sharding import PartitionSpec as P


def tanh_layer(value, tangents, laplacian, w_full, bias):
    feat_index = lax.axis_index("feat")
    half_width = value.shape[1]
    count_w, count_t = (tangents.shape[0], tangents.shape[1])
    stacked = jnp.stack([value, laplacian])
    w_rows = lax.dynamic_slice_in_dim(w_full, feat_index * half_width, half_width, 0)
    partial_vl = jnp.einsum("kbd,de->kbe", stacked, w_rows, preferred_element_type=jnp.float32)
    partial_grad = jnp.dot(
        tangents.reshape(count_w * count_t, half_width), w_rows, preferred_element_type=jnp.float32
    ).reshape(count_w, count_t, w_full.shape[1])
    summed, grad_pre = (
        lax.psum_scatter(partial_vl, "feat", scatter_dimension=2, tiled=True),
        lax.psum_scatter(partial_grad, "feat", scatter_dimension=2, tiled=True),
    )
    pre_act = summed[0] + bias
    lap_pre = summed[1]
    hidden = jnp.tanh(pre_act)
    slope = 1.0 - hidden * hidden
    bend = -2.0 * hidden * slope
    return (hidden, slope, bend, grad_pre, lap_pre)


def own_half(vector, half_width):
    return lax.dynamic_slice_in_dim(vector, lax.axis_index("feat") * half_width, half_width, 0)


def per_device(value_in, tang_in, lap_in, w_first, b_first, w_second, b_second, readout):
    full_first, full_second = (
        lax.all_gather(w_first, ("walker", "tangent", "feat"), axis=0, tiled=True),
        lax.all_gather(w_second, ("walker", "tangent", "feat"), axis=0, tiled=True),
    )
    half_width = value_in.shape[1]
    value_start, lap_start, tangents_in = (value_in, lap_in, tang_in)
    bias_one = own_half(b_first, half_width)
    bias_two = own_half(b_second, half_width)
    read_weights = own_half(readout, half_width)
    hidden, slope, bend, grad_pre, lap_pre = tanh_layer(
        value_start, tangents_in, lap_start, full_first, bias_one
    )
    curv_first = lax.psum(jnp.sum(grad_pre * grad_pre, axis=1), "tangent")
    value_two = hidden.astype(jnp.bfloat16)
    tang_two = (slope[:, None, :] * grad_pre).astype(jnp.bfloat16)
    lap_two = (slope * lap_pre + bend * curv_first).astype(jnp.bfloat16)
    hidden, slope, bend, grad_pre, lap_pre = tanh_layer(
        value_two, tang_two, lap_two, full_second, bias_two
    )
    amp_part = jnp.sum(read_weights * hidden, axis=-1)
    grad_part = jnp.sum(grad_pre * (read_weights * slope)[:, None, :], axis=-1)
    local_squares = jnp.sum(grad_pre * grad_pre, axis=1)
    curv_second = lax.psum(local_squares, "tangent")
    lap_part = jnp.sum(read_weights * (slope * lap_pre + bend * curv_second), axis=-1)
    log_amplitude, gradient, laplace = lax.psum((amp_part, grad_part, lap_part), "feat")
    squares = lax.psum(jnp.sum(gradient * gradient, axis=-1), "tangent")
    kinetic = -0.5 * (laplace + squares)
    return (log_amplitude, gradient, kinetic)


def solution(mesh):
    placed = (
        P("walker", "feat"),
        P("walker", "tangent", "feat"),
        P("walker", "feat"),
        P(("walker", "tangent", "feat"), None),
        P(),
        P(("walker", "tangent", "feat"), None),
        P(),
        P(),
    )
    return jax.shard_map(
        per_device,
        mesh=mesh,
        in_specs=placed,
        out_specs=(P("walker"), P("walker", "tangent"), P("walker")),
        check_vma=False,
    )
```

profile of v0, /device:TPU:1, one launch (start us, length us, event | category | flops | bytes accessed | tf_op | source)
XLA Modules:
  0.0 270.8 jit_solution(8628064673603538799)
XLA Ops:
  7.2 0.0 copy-start
  7.2 0.0 reduce-scatter.5.cloned.1.call-start
  7.2 73.3 %all-gather = bf16[256,2,512]{2,1,0:T(2,128)(2,1)S(1)} all-gather(bf16[1,2,512]{2,1,0:T(2,128)(2,1)} %bitcast.67), channel_id=1, replica_groups=mesh['walker'=16,'tangent'=8,'feat'=2] {'walker','tangent','feat'}, dimensions={0}, use_global_device_ids=true | all-gather | bytes 526336 | tf_op jit(solution)/shard_map/all_gather | solution.py:35
  80.5 0.2 reshape.72
  80.7 1.6 fusion.5
  82.3 0.0 reduce-scatter.5.cloned.1.call-update
  82.3 0.0 reduce-scatter.7.cloned.1.call-start
  82.4 0.0 copy-done
  82.4 3.7 %convolution_bitcast_fusion = f32[3072,512]{0,1:T(8,128)} fusion(bf16[3072,256]{1,0:T(8,128)(2,1)S(1)} %bitcast.63, bf16[512,512]{1,0:T(8,128)(2,1)S(1)} %reshape.72, s32[]{:T(128)S(6)} %select_n.2), kind=kOutput, calls=%fused_computation | convolution fusion | flops 805306368 | bytes 8126468 | tf_op jit(solution)/shard_map/dot_general | solution.py:14
  86.1 6.6 %copy.13 = f32[3072,512]{1,0:T(8,128)} copy(f32[3072,512]{0,1:T(8,128)} %convolution_bitcast_fusion) | data formatting | bytes 12582912 | tf_op jit(solution)/shard_map/dot_general | solution.py:14
  92.7 0.0 copy-start.5
  92.7 0.0 copy-start.4
  92.7 0.0 reduce-scatter.7.cloned.1.call-update
  92.7 0.0 reduce-scatter.9.cloned.1.call-start
  92.8 0.6 copy-done.5
  93.4 0.1 dynamic_slice.17
  93.5 0.0 copy-done.4
  93.5 65.6 %all-gather.1 = bf16[256,2,512]{2,1,0:T(2,128)(2,1)S(1)} all-gather(bf16[1,2,512]{2,1,0:T(2,128)(2,1)S(1)} %bitcast.68), channel_id=1, replica_groups=mesh['walker'=16,'tangent'=8,'feat'=2] {'walker','tangent','feat'}, dimensions={0}, use_global_device_ids=true | all-gather | bytes 526336 | tf_op jit(solution)/shard_map/all_gather | solution.py:36
  159.1 0.2 reshape.74
  159.3 0.0 reduce-scatter.5.cloned.1.call-done
  159.3 0.0 copy-start.1
  159.3 0.8 tanh_convert_fusion
  160.2 0.0 reduce-scatter.7.cloned.1.call-done
  160.2 2.2 multiply_reduce_fusion.2
  162.4 22.1 %psum.42 = f32[32,256]{1,0:T(8,128)S(1)} all-reduce(f32[32,256]{1,0:T(8,128)S(1)} %multiply_reduce_fusion.2), channel_id=1, replica_groups=mesh['walker'=16,'tangent'=8,'feat'=2] {'tangent'}, use_global_device_ids=true, to_apply=%region_3.0 | all-reduce | flops 8192 | bytes 65536 | tf_op jit(solution)/shard_map/psum | solution.py:46
  184.6 0.0 copy-done.1
  184.6 0.8 fusion.3
  185.4 0.0 reduce-scatter.9.cloned.1.call-update
  185.4 0.0 reduce-scatter.11.cloned.1.call-start
  185.5 5.5 %fusion = f32[32,96,512]{2,1,0:T(8,128)} fusion(f32[32,96,256]{2,1,0:T(8,128)} %reduce-scatter.7.cloned.1.call-done, f32[32,256]{1,0:T(8,128)S(1)} %get-tuple-element.11, bf16[512,512]{1,0:T(8,128)(2,1)S(1)} %reshape.74, s32[]{:T(128)S(6)} %select_n.2), kind=kOutput, calls=%fused_computation.5 | convolution fusion | flops 806879232 | bytes 9732100 | tf_op jit(solution)/shard_map/dot_general | solution.py:14
  191.0 0.0 copy-start.6
  191.0 0.0 reduce-scatter.11.cloned.1.call-update
  191.1 0.7 copy-done.6
  191.7 0.1 dynamic_slice.15
  191.8 0.0 copy-done.7
  191.8 0.1 dynamic_slice.19
  191.9 9.7 %reduce-scatter.9.cloned.1.call-done = f32[2,32,256]{2,1,0:T(8,128)} async-done(((f32[2,32,512]{2,1,0:T(8,128)}), f32[2,32,256]{2,1,0:T(8,128)}) %reduce-scatter.9.cloned.1.call-update) | async-done | bytes 65552 | tf_op jit(solution)/shard_map/reduce_scatter | solution.py:18
  201.6 0.8 fusion.27
  202.4 21.9 %reduce-scatter.11.cloned.1.call-done = f32[32,96,256]{2,1,0:T(8,128)} async-done(((f32[32,96,512]{2,1,0:T(8,128)}), f32[32,96,256]{2,1,0:T(8,128)}) %reduce-scatter.11.cloned.1.call-update) | async-done | bytes 3145744 | tf_op jit(solution)/shard_map/reduce_scatter | solution.py:19
  224.4 2.5 multiply_reduce_fusion
  226.9 3.6 %psum.44 = f32[32,96]{1,0:T(8,128)S(1)} all-reduce(f32[32,96]{1,0:T(8,128)S(1)} %get-tuple-element.4), channel_id=1, replica_groups=mesh['walker'=16,'tangent'=8,'feat'=2] {'feat'}, use_global_device_ids=true, to_apply=%region_9.0 | all-reduce | flops 3072 | bytes 24576 | tf_op jit(solution)/shard_map/psum | solution.py:58
  230.5 0.1 multiply_reduce_fusion.4
  230.6 23.2 %all-reduce = (f32[32,256]{1,0:T(8,128)S(1)}, f32[32]{0:T(128)S(1)}) all-reduce(f32[32,256]{1,0:T(8,128)S(1)} %get-tuple-element.3, f32[32]{0:T(128)S(1)} %multiply_reduce_fusion.4), channel_id=1, replica_groups=mesh['walker'=16,'tangent'=8,'feat'=2] {'tangent'}, use_global_device_ids=true, to_apply=%region_11.0 | all-reduce | flops 8224 | bytes 65792 | tf_op jit(solution)/shard_map/psum | solution.py:56
  253.8 0.0 copy-done.2
  253.8 0.1 fusion.14
  253.9 9.9 %all-reduce.1 = (f32[32]{0:T(128)}, f32[32]{0:T(128)S(1)}) all-reduce(f32[32]{0:T(128)S(1)} %get-tuple-element.6, f32[32]{0:T(128)S(1)} %get-tuple-element.5), channel_id=1, replica_groups=mesh['walker'=16,'tangent'=8,'feat'=2] {'feat'}, use_global_device_ids=true, to_apply=%region_6.0 | all-reduce | flops 64 | bytes 512 | tf_op jit(solution)/shard_map/psum | solution.py:58
  263.8 0.5 add_multiply_fusion
  264.3 0.0 copy-done.3
  (4 shorter events, 0.0 us)
Async XLA Ops:
  7.2 75.2 %copy-start = (bf16[32,96,256]{2,1,0:T(8,128)(2,1)S(1)}, bf16[32,96,256]{2,1,0:T(8,128)(2,1)}, u32[]{:S(2)}) copy-start(bf16[32,96,256]{2,1,0:T(8,128)(2,1)} %param.9) | copy-start | bytes 4718596
  7.2 152.1 %reduce-scatter.5.cloned.1.call-start = ((), (), s32[]{:S(2)}) async-start(), calls=%async_computation.4 | async-start | bytes 196608 | tf_op jit(solution)/shard_map/reduce_scatter | solution.py:18
  82.3 77.9 %reduce-scatter.7.cloned.1.call-start = ((), (), s32[]{:S(2)}) async-start(), calls=%async_computation.5 | async-start | bytes 9437184 | tf_op jit(solution)/shard_map/reduce_scatter | solution.py:19
  92.7 0.7 copy-start.5
  92.7 0.8 copy-start.4
  92.7 108.9 %reduce-scatter.9.cloned.1.call-start = ((), (), s32[]{:S(2)}) async-start(), calls=%async_computation.6 | async-start | bytes 196608 | tf_op jit(solution)/shard_map/reduce_scatter | solution.py:18
  159.3 25.2 %copy-start.1 = (f32[2,32,256]{2,1,0:T(8,128)S(1)}, f32[2,32,256]{2,1,0:T(8,128)}, u32[]{:S(2)}) copy-start(f32[2,32,256]{2,1,0:T(8,128)} %reduce-scatter.5.cloned.1.call-done) | copy-start | bytes 196612
  185.4 38.9 %reduce-scatter.11.cloned.1.call-start = ((), (), s32[]{:S(2)}) async-start(), calls=%async_computation.7 | async-start | bytes 9437184 | tf_op jit(solution)/shard_map/reduce_scatter | solution.py:19
  191.0 0.7 copy-start.6
  191.0 0.8 copy-start.7
  201.6 52.2 %copy-start.2 = (f32[2,32,256]{2,1,0:T(8,128)S(1)}, f32[2,32,256]{2,1,0:T(8,128)}, u32[]{:S(2)}) copy-start(f32[2,32,256]{2,1,0:T(8,128)} %reduce-scatter.9.cloned.1.call-done) | copy-start | bytes 196612
  230.5 33.8 %copy-start.3 = (f32[32,96]{1,0:T(8,128)}, f32[32,96]{1,0:T(8,128)S(1)}, u32[]{:S(2)}) copy-start(f32[32,96]{1,0:T(8,128)S(1)} %psum.44) | copy-start | bytes 36868
Sparse Core Ops, SparseCore 0:
  82.5 9.7 reduce-scatter.4
  94.8 20.2 reduce-scatter.6
  185.6 15.9 reduce-scatter.8
  204.0 20.3 reduce-scatter.10
where the time goes:
time: 271 us
  blocking collectives  198 us (73%)
  waiting for transfers between devices  31.8 us (12%)
  between operations  13.9 us (5%)
  matrix products  11.6 us (4%)
  local copies, waits for them, and re-layouts  8.51 us (3%)
  other arithmetic  7.18 us (3%)
    all_gather x1, blocking collectives, per_device(): lax.all_gather(w_first, ('walker', 'tangent', 'feat'), axis=0, tiled=True)  73.3 us
    all_gather x1, blocking collectives, per_device(): lax.all_gather(w_second, ('walker', 'tangent', 'feat'), axis=0, tiled=True)  65.6 us
    psum x1, blocking collectives, per_device(): curv_second = lax.psum(local_squares, 'tangent')  23.2 us
    psum x1, blocking collectives, per_device(): curv_first = lax.psum(jnp.sum(grad_pre * grad_pre, axis=1), 'tangent')  22.1 us
    reduce_scatter x2, waiting for transfers between devices, tanh_layer(): lax.psum_scatter(partial_grad, 'feat', scatter_dimension=2, tiled=True)  21.9 us
    psum x2, blocking collectives, per_device(): lax.psum((amp_part, grad_part, lap_part), 'feat')  13.5 us
    reduce_scatter x2, waiting for transfers between devices, tanh_layer(): lax.psum_scatter(partial_vl, 'feat', scatter_dimension=2, tiled=True)  9.74 us
    dot_general x2, matrix products, tanh_layer(): jnp.dot(tangents.reshape(count_w * count_t, half_width), w_rows, preferre...  9.24 us
  transfers between devices with their start and end apart: 4, of which 2 were waited for; matrix products, arithmetic and copies ran while one was open for 7% of the time, Pallas kernels for 0%

commit v1 on v0

--- a/solution.py
+++ b/solution.py
@@ -33,7 +33,15 @@
 def per_device(value_in, tang_in, lap_in, w_first, b_first, w_second, b_second, readout):
     full_first, full_second = (
         lax.all_gather(w_first, ("walker", "tangent", "feat"), axis=0, tiled=True),
-        lax.all_gather(w_second, ("walker", "tangent", "feat"), axis=0, tiled=True),
+        jnp.concatenate(
+            lax.all_to_all(
+                jnp.stack([w_second] * lax.axis_size(("walker", "tangent", "feat"))),
+                ("walker", "tangent", "feat"),
+                0,
+                0,
+            ),
+            axis=0,
+        ),
     )
     half_width = value_in.shape[1]
     value_start, lap_start, tangents_in = (value_in, lap_in, tang_in)

time: 271 us -> 233 us (0.86)
  blocking collectives: 198 us -> 131 us
  waiting for transfers between devices: 31.8 us -> 51.3 us
  starting transfers between devices: 0.16 us -> 8.1 us
    all_gather x1 -> x0, blocking collectives: 65.6 us -> none  [per_device(): lax.all_gather(w_second, ('walker', 'tangent', 'feat'), axis=0, tiled=True)]
    all_to_all x0 -> x1, waiting for transfers between devices: none -> 20.4 us  [per_device(): lax.all_to_all(jnp.stack([w_second] * lax.axis_size(('walker', 'tangent',...]
    all_to_all x0 -> x1, starting transfers between devices: none -> 7.94 us  [per_device(): lax.all_to_all(jnp.stack([w_second] * lax.axis_size(('walker', 'tangent',...]
  transfers between devices with their start and end apart: 4 -> 5, of which waited for: 2 -> 3; matrix products, arithmetic and copies ran while one was open for 7% -> 8% of each run, Pallas kernels for 0% -> 0%
where the time goes in v1:
time: 233 us; the launch traced here: 232 us
  blocking collectives  131 us (56%)
  waiting for transfers between devices  51.3 us (22%)
  between operations  13.9 us (6%)
  matrix products  11.6 us (5%)
  local copies, waits for them, and re-layouts  9.63 us (4%)
  starting transfers between devices  8.1 us (3%)
  other arithmetic  7.19 us (3%)
    all_gather x1, blocking collectives, per_device(): lax.all_gather(w_first, ('walker', 'tangent', 'feat'), axis=0, tiled=True)  73.3 us
    psum x1, blocking collectives, per_device(): curv_second = lax.psum(local_squares, 'tangent')  23.1 us
    reduce_scatter x2, waiting for transfers between devices, tanh_layer(): lax.psum_scatter(partial_grad, 'feat', scatter_dimension=2, tiled=True)  21.9 us
    psum x1, blocking collectives, per_device(): curv_first = lax.psum(jnp.sum(grad_pre * grad_pre, axis=1), 'tangent')  20.6 us
    all_to_all x1, waiting for transfers between devices, per_device(): lax.all_to_all(jnp.stack([w_second] * lax.axis_size(('walker', 'tangent',...  20.4 us
    psum x2, blocking collectives, per_device(): lax.psum((amp_part, grad_part, lap_part), 'feat')  13.5 us
    dot_general x2, matrix products, tanh_layer(): jnp.dot(tangents.reshape(count_w * count_t, half_width), w_rows, preferre...  9.24 us
    reduce_scatter x2, waiting for transfers between devices, tanh_layer(): lax.psum_scatter(partial_vl, 'feat', scatter_dimension=2, tiled=True)  8.91 us
  transfers between devices with their start and end apart: 5, of which 3 were waited for; matrix products, arithmetic and copies ran while one was open for 8% of the time, Pallas kernels for 0%

profile of v1, /device:TPU:1, one launch (start us, length us, event | category | flops | bytes accessed | tf_op | source)
XLA Modules:
  0.0 232.3 jit_solution(4439013841642403656)
XLA Ops:
  7.2 0.0 copy-start
  7.2 0.0 reduce-scatter.5.cloned.1.call-start
  7.2 73.3 %all-gather = bf16[256,2,512]{2,1,0:T(2,128)(2,1)S(1)} all-gather(bf16[1,2,512]{2,1,0:T(2,128)(2,1)} %bitcast.66), channel_id=1, replica_groups=mesh['walker'=16,'tangent'=8,'feat'=2] {'walker','tangent','feat'}, dimensions={0}, use_global_device_ids=true | all-gather | bytes 526336 | tf_op jit(solution)/shard_map/all_gather | solution.py:35
  80.5 0.2 reshape.78
  80.7 1.6 fusion.5
  82.3 0.0 reduce-scatter.5.cloned.1.call-update
  82.3 0.0 reduce-scatter.7.cloned.1.call-start
  82.4 0.0 copy-done
  82.4 3.7 %convolution_bitcast_fusion = f32[3072,512]{0,1:T(8,128)} fusion(bf16[3072,256]{1,0:T(8,128)(2,1)S(1)} %bitcast.62, bf16[512,512]{1,0:T(8,128)(2,1)S(1)} %reshape.78, s32[]{:T(128)S(6)} %select_n.2), kind=kOutput, calls=%fused_computation | convolution fusion | flops 805306368 | bytes 8126468 | tf_op jit(solution)/shard_map/dot_general | solution.py:14
  86.1 6.6 %copy.13 = f32[3072,512]{1,0:T(8,128)} copy(f32[3072,512]{0,1:T(8,128)} %convolution_bitcast_fusion) | data formatting | bytes 12582912 | tf_op jit(solution)/shard_map/dot_general | solution.py:14
  92.7 0.0 copy-start.4
  92.7 0.0 copy-start.5
  92.7 0.0 reduce-scatter.7.cloned.1.call-update
  92.7 0.7 copy-done.4
  93.4 1.1 stack.17
  94.4 7.9 %all-to-all-start = ((bf16[256,2,512]{2,1,0:T(2,128)(2,1)}), bf16[256,2,512]{2,1,0:T(2,128)(2,1)S(1)}, u32[]{:S(2)}, u32[]{:S(2)}) async-start(bf16[256,2,512]{2,1,0:T(2,128)(2,1)} %stack.17), calls=%async_computation.2 | async-start | bytes 1048576 | tf_op jit(solution)/shard_map/all_to_all | solution.py:37
  102.4 0.0 reduce-scatter.9.cloned.1.call-start
  102.4 0.0 copy-done.5
  102.5 0.1 dynamic_slice.17
  102.5 0.0 reduce-scatter.5.cloned.1.call-done
  102.5 0.8 tanh_convert_fusion
  103.4 20.4 %all-to-all-done = bf16[256,2,512]{2,1,0:T(2,128)(2,1)S(1)} async-done(((bf16[256,2,512]{2,1,0:T(2,128)(2,1)}), bf16[256,2,512]{2,1,0:T(2,128)(2,1)S(1)}, u32[]{:S(2)}, u32[]{:S(2)}) %all-to-all-start) | async-done | bytes 524320 | tf_op jit(solution)/shard_map/all_to_all | solution.py:37
  123.8 0.2 reshape.76
  124.0 0.0 reduce-scatter.7.cloned.1.call-done
  124.0 2.2 multiply_reduce_fusion.2
  126.2 20.6 %psum.42 = f32[32,256]{1,0:T(8,128)S(1)} all-reduce(f32[32,256]{1,0:T(8,128)S(1)} %multiply_reduce_fusion.2), channel_id=1, replica_groups=mesh['walker'=16,'tangent'=8,'feat'=2] {'tangent'}, use_global_device_ids=true, to_apply=%region_3.0 | all-reduce | flops 8192 | bytes 65536 | tf_op jit(solution)/shard_map/psum | solution.py:54
  146.8 0.0 copy-done.1
  146.9 0.8 fusion.3
  147.7 0.0 reduce-scatter.9.cloned.1.call-update
  147.7 0.0 reduce-scatter.11.cloned.1.call-start
  147.8 5.5 %fusion = f32[32,96,512]{2,1,0:T(8,128)} fusion(f32[32,96,256]{2,1,0:T(8,128)} %reduce-scatter.7.cloned.1.call-done, f32[32,256]{1,0:T(8,128)S(1)} %get-tuple-element.11, bf16[512,512]{1,0:T(8,128)(2,1)S(1)} %reshape.76, s32[]{:T(128)S(6)} %select_n.2), kind=kOutput, calls=%fused_computation.5 | convolution fusion | flops 806879232 | bytes 9732100 | tf_op jit(solution)/shard_map/dot_general | solution.py:14
  153.3 0.0 reduce-scatter.11.cloned.1.call-update
  153.3 0.7 copy-done.6
  154.0 0.1 dynamic_slice.15
  154.1 0.0 copy-done.7
  154.1 0.1 dynamic_slice.19
  154.2 8.9 %reduce-scatter.9.cloned.1.call-done = f32[2,32,256]{2,1,0:T(8,128)} async-done(((f32[2,32,512]{2,1,0:T(8,128)}), f32[2,32,256]{2,1,0:T(8,128)}) %reduce-scatter.9.cloned.1.call-update) | async-done | bytes 65552 | tf_op jit(solution)/shard_map/reduce_scatter | solution.py:18
  163.1 0.8 fusion.27
  163.9 21.9 %reduce-scatter.11.cloned.1.call-done = f32[32,96,256]{2,1,0:T(8,128)} async-done(((f32[32,96,512]{2,1,0:T(8,128)}), f32[32,96,256]{2,1,0:T(8,128)}) %reduce-scatter.11.cloned.1.call-update) | async-done | bytes 3145744 | tf_op jit(solution)/shard_map/reduce_scatter | solution.py:19
  185.8 2.5 %multiply_reduce_fusion = (f32[32,256]{1,0:T(8,128)S(1)}, f32[32,96]{1,0:T(8,128)S(1)}) fusion(f32[32,96,256]{2,1,0:T(8,128)} %reduce-scatter.11.cloned.1.call-done, f32[32,256]{1,0:T(8,128)S(1)} %fusion.27), kind=kLoop, calls=%fused_computation.1 | loop fusion | flops 3134464 | bytes 3223552 | tf_op jit(solution)/shard_map/reduce_sum | solution.py:63
  188.3 3.6 %psum.44 = f32[32,96]{1,0:T(8,128)S(1)} all-reduce(f32[32,96]{1,0:T(8,128)S(1)} %get-tuple-element.4), channel_id=1, replica_groups=mesh['walker'=16,'tangent'=8,'feat'=2] {'feat'}, use_global_device_ids=true, to_apply=%region_9.0 | all-reduce | flops 3072 | bytes 24576 | tf_op jit(solution)/shard_map/psum | solution.py:66
  191.9 0.1 multiply_reduce_fusion.4
  192.0 23.1 %all-reduce = (f32[32,256]{1,0:T(8,128)S(1)}, f32[32]{0:T(128)S(1)}) all-reduce(f32[32,256]{1,0:T(8,128)S(1)} %get-tuple-element.3, f32[32]{0:T(128)S(1)} %multiply_reduce_fusion.4), channel_id=1, replica_groups=mesh['walker'=16,'tangent'=8,'feat'=2] {'tangent'}, use_global_device_ids=true, to_apply=%region_11.0 | all-reduce | flops 8224 | bytes 65792 | tf_op jit(solution)/shard_map/psum | solution.py:64
  215.2 0.0 copy-done.2
  215.2 0.1 fusion.14
  215.3 9.9 %all-reduce.1 = (f32[32]{0:T(128)}, f32[32]{0:T(128)S(1)}) all-reduce(f32[32]{0:T(128)S(1)} %get-tuple-element.6, f32[32]{0:T(128)S(1)} %get-tuple-element.5), channel_id=1, replica_groups=mesh['walker'=16,'tangent'=8,'feat'=2] {'feat'}, use_global_device_ids=true, to_apply=%region_6.0 | all-reduce | flops 64 | bytes 512 | tf_op jit(solution)/shard_map/psum | solution.py:66
  225.2 0.5 add_multiply_fusion
  225.7 0.0 copy-done.3
  (6 shorter events, 0.0 us)
Async XLA Ops:
  7.2 75.2 %copy-start = (bf16[32,96,256]{2,1,0:T(8,128)(2,1)S(1)}, bf16[32,96,256]{2,1,0:T(8,128)(2,1)}, u32[]{:S(2)}) copy-start(bf16[32,96,256]{2,1,0:T(8,128)(2,1)} %param.9) | copy-start | bytes 4718596
  7.2 95.4 %reduce-scatter.5.cloned.1.call-start = ((), (), s32[]{:S(2)}) async-start(), calls=%async_computation.5 | async-start | bytes 196608 | tf_op jit(solution)/shard_map/reduce_scatter | solution.py:18
  82.3 41.7 %reduce-scatter.7.cloned.1.call-start = ((), (), s32[]{:S(2)}) async-start(), calls=%async_computation.6 | async-start | bytes 9437184 | tf_op jit(solution)/shard_map/reduce_scatter | solution.py:19
  92.7 0.7 copy-start.4
  92.7 9.7 %copy-start.5 = (f32[512]{0:T(512)S(1)}, f32[512]{0:T(512)}, u32[]{:S(2)}) copy-start(f32[512]{0:T(512)} %param.12) | copy-start | bytes 6148
  94.4 29.3 %all-to-all-start = ((bf16[256,2,512]{2,1,0:T(2,128)(2,1)}), bf16[256,2,512]{2,1,0:T(2,128)(2,1)S(1)}, u32[]{:S(2)}, u32[]{:S(2)}) async-start(bf16[256,2,512]{2,1,0:T(2,128)(2,1)} %stack.17), calls=%async_computation.2 | async-start | bytes 1048576 | tf_op jit(solution)/shard_map/all_to_all | solution.py:37
  102.4 60.7 %reduce-scatter.9.cloned.1.call-start = ((), (), s32[]{:S(2)}) async-start(), calls=%async_computation.7 | async-start | bytes 196608 | tf_op jit(solution)/shard_map/reduce_scatter | solution.py:18
  102.5 44.3 %copy-start.1 = (f32[2,32,256]{2,1,0:T(8,128)S(1)}, f32[2,32,256]{2,1,0:T(8,128)}, u32[]{:S(2)}) copy-start(f32[2,32,256]{2,1,0:T(8,128)} %reduce-scatter.5.cloned.1.call-done) | copy-start | bytes 196612
  147.7 38.1 %reduce-scatter.11.cloned.1.call-start = ((), (), s32[]{:S(2)}) async-start(), calls=%async_computation.8 | async-start | bytes 9437184 | tf_op jit(solution)/shard_map/reduce_scatter | solution.py:19
  153.3 0.7 copy-start.6
  153.3 0.8 copy-start.7
  163.1 52.1 %copy-start.2 = (f32[2,32,256]{2,1,0:T(8,128)S(1)}, f32[2,32,256]{2,1,0:T(8,128)}, u32[]{:S(2)}) copy-start(f32[2,32,256]{2,1,0:T(8,128)} %reduce-scatter.9.cloned.1.call-done) | copy-start | bytes 196612
  191.9 33.8 %copy-start.3 = (f32[32,96]{1,0:T(8,128)}, f32[32,96]{1,0:T(8,128)S(1)}, u32[]{:S(2)}) copy-start(f32[32,96]{1,0:T(8,128)S(1)} %psum.44) | copy-start | bytes 36868
Sparse Core Ops, SparseCore 0:
  82.5 9.7 reduce-scatter.4
  94.8 20.2 reduce-scatter.6
  147.8 15.1 reduce-scatter.8
  165.5 20.2 reduce-scatter.10
